TPU v7x, 512 devices: a whole 4x4x16 slice. The times are simulated.
512 devices in a mesh: dp: 32 (over y, x, core), seq: 16 (over z).
Axes of the slice: x: 4, y: 4, z: 16, core: 2. Of those that a mesh axis runs over, the one named last changes fastest.
Arguments:
- tokens: bfloat16 [64, 4096, 768], P('dp', 'seq'), may hold values from -6 to 6
- norm_gain: float32 [768], replicated, may hold values from 0.1 to 1.9
- dilated_weight: bfloat16 [3, 768, 384], P(None, None, 'seq'), may hold values from -0.125 to 0.125
- output_weight: bfloat16 [384, 768], P(None, 'seq'), may hold values from -0.3125 to 0.3125
- cotangent: bfloat16 [64, 4096, 768], P('dp', 'seq'), may hold values from -6 to 6
Outputs:
- block_output: bfloat16 [64, 4096, 768], P('dp', 'seq')
- token_input_gradient: bfloat16 [64, 4096, 768], P('dp', 'seq')
- dilated_gradient: float32 [3, 768, 384], P(None, None, 'seq')
- output_gradient: float32 [384, 768], P(None, 'seq')
- gain_gradient: float32 [768], P('seq')
All inputs are finite; a program needn't handle non-finite values.
Results may differ from a plain program's by a relative error of at most 0.017.
Values may be sent and summed in bfloat16 or wider, within the bound.
No kernel may reach another device: no remote copies, remote signals or barrier semaphores. Data moves between devices by JAX's collectives and lax.ppermute only.
A program may use at most 64 MiB of HBM per device.

v0:
```python
import jax
import jax.numpy as jnp
from jax import lax
from jax.sharding import PartitionSpec as P

DILATION_STEP = 64
gelu_scale = 0.7978845608
cubic_term = 0.044715
epsilon = 1e-06


def extended(value, sides, width):
    for axis, dim in sides:
        size, length = (lax.axis_size(axis), value.shape[dim])
        up = [(i, (i + 1) % size) for i in range(size - 1)]
        down = [(j, i) for i, j in up]
        last = lax.slice_in_dim(value, length - width, length, axis=dim)
        first = lax.slice_in_dim(value, 0, width, axis=dim)
        before = lax.ppermute(last, axis, up)
        after = lax.ppermute(first, axis, down)
        value = jnp.concatenate([before, value, after], axis=dim)
    return value


def activate(value):
    inner = jnp.tanh(gelu_scale * (value + cubic_term * value * value * value))
    return 0.5 * value * (1.0 + inner)


def derivative(value):
    inner = jnp.tanh(gelu_scale * (value + cubic_term * value * value * value))
    return 0.5 * (1.0 + inner) + 0.5 * value * (1.0 - inner * inner) * gelu_scale * (
        1.0 + 3.0 * cubic_term * value * value
    )


def combine_block_parts(received, sequence_number):
    return jnp.sum(
        received.reshape(sequence_number, received.shape[0] // sequence_number, received.shape[1]),
        axis=0,
    )


def on_device(tokens, norm_gain, dilated_weight, output_weight, cotangent):
    seqs_here, local_bins, channel_count = tokens.shape
    sequence_number = lax.axis_size("seq")
    collected_dilated, collected_output = (
        lax.all_gather(
            dilated_weight.reshape(3 * channel_count, dilated_weight.shape[2]),
            "seq",
            axis=1,
            tiled=True,
        ),
        lax.all_gather(output_weight, "seq", axis=1, tiled=True),
    )
    hidden_width = collected_dilated.shape[1]
    kernel_taps = collected_dilated.reshape(3, channel_count, hidden_width)
    as_float = tokens.astype(jnp.float32)
    inverse_rms = lax.rsqrt(jnp.mean(as_float * as_float, axis=-1, keepdims=True) + epsilon)
    normed = as_float * inverse_rms * norm_gain
    gelu_activated = activate(normed).astype(jnp.bfloat16)
    padded_input = extended(gelu_activated, (("seq", 1),), DILATION_STEP)
    dilated_sum = jnp.zeros((seqs_here * local_bins, hidden_width), jnp.float32)
    for tap_index in range(3):
        dilated_sum = dilated_sum + jnp.dot(
            padded_input[
                :, tap_index * DILATION_STEP : tap_index * DILATION_STEP + local_bins
            ].reshape(-1, channel_count),
            kernel_taps[tap_index],
            preferred_element_type=jnp.float32,
        )
    dilated_sum = dilated_sum.reshape(seqs_here, local_bins, hidden_width)
    hidden = activate(dilated_sum).astype(jnp.bfloat16)
    hidden_rows = hidden.reshape(-1, hidden_width)
    projected = jnp.dot(hidden_rows, collected_output, preferred_element_type=jnp.float32)
    residual_output = (as_float + projected.reshape(seqs_here, local_bins, channel_count)).astype(
        jnp.bfloat16
    )
    cot_rows = cotangent.reshape(-1, channel_count)
    hidden_cot = jnp.einsum(
        "nc,hc->nh", cot_rows, collected_output, preferred_element_type=jnp.float32
    ).astype(jnp.bfloat16)
    output_piece = jnp.einsum(
        "nh,nc->hc", hidden_rows, cot_rows, preferred_element_type=jnp.float32
    )
    cotangent_sum = (
        hidden_cot.reshape(seqs_here, local_bins, hidden_width).astype(jnp.float32)
        * derivative(dilated_sum)
    ).astype(jnp.bfloat16)
    padded_cotangent = extended(cotangent_sum, (("seq", 1),), DILATION_STEP)
    act_cot = jnp.zeros((seqs_here * local_bins, channel_count), jnp.float32)
    dilated_pieces = []
    for tap_index in range(3):
        start_offset = (2 - tap_index) * DILATION_STEP
        piece = padded_cotangent[:, start_offset : start_offset + local_bins].reshape(
            -1, hidden_width
        )
        act_cot = act_cot + jnp.einsum(
            "nh,ch->nc", piece, kernel_taps[tap_index], preferred_element_type=jnp.float32
        )
        dilated_pieces.append(
            jnp.einsum(
                "blc,blh->ch",
                padded_input[:, tap_index * DILATION_STEP : tap_index * DILATION_STEP + local_bins],
                cotangent_sum,
                preferred_element_type=jnp.float32,
            )
        )
    act_cot = act_cot.astype(jnp.bfloat16).reshape(seqs_here, local_bins, channel_count)
    normed_cot = act_cot.astype(jnp.float32) * derivative(normed)
    scaled_cot = norm_gain * normed_cot
    token_cotangent = (
        cotangent.astype(jnp.float32)
        + inverse_rms * scaled_cot
        - as_float * inverse_rms**3 * jnp.mean(scaled_cot * as_float, axis=-1, keepdims=True)
    )
    token_cotangent = token_cotangent.astype(jnp.bfloat16)
    gain_piece = jnp.sum(normed_cot * as_float * inverse_rms, axis=(0, 1))
    dilated_piece = jnp.stack(dilated_pieces).reshape(3 * channel_count, hidden_width)
    incoming_dilated, incoming_output, incoming_gain = (
        lax.all_to_all(dilated_piece, "seq", split_axis=1, concat_axis=0, tiled=True),
        lax.all_to_all(output_piece, "seq", split_axis=1, concat_axis=0, tiled=True),
        lax.all_to_all(
            gain_piece.reshape(1, channel_count), "seq", split_axis=1, concat_axis=0, tiled=True
        ),
    )
    dilated_weight_portion = combine_block_parts(incoming_dilated, sequence_number)
    output_weight_portion = combine_block_parts(incoming_output, sequence_number)
    gain_share = combine_block_parts(incoming_gain, sequence_number)
    dilated_total, output_total, gain_total = lax.psum(
        (dilated_weight_portion, output_weight_portion, gain_share), "dp"
    )
    scale_factor = 1.0 / (seqs_here * lax.axis_size("dp"))
    return (
        residual_output,
        token_cotangent,
        (dilated_total * scale_factor).reshape(3, channel_count, -1),
        output_total * scale_factor,
        (gain_total * scale_factor).reshape(-1),
    )


def solution(mesh):
    in_specs = (
        P("dp", "seq", None),
        P(),
        P(None, None, "seq"),
        P(None, "seq"),
        P("dp", "seq", None),
    )
    out_specs = (
        P("dp", "seq", None),
        P("dp", "seq", None),
        P(None, None, "seq"),
        P(None, "seq"),
        P("seq"),
    )
    return jax.shard_map(
        on_device, mesh=mesh, in_specs=in_specs, out_specs=out_specs, check_vma=False
    )
```

profile of v0, /device:TPU:1, one launch (start us, length us, event | category | flops | bytes accessed | tf_op | source)
XLA Modules:
  0.0 478.6 jit_solution(10501041938618014832)
XLA Ops:
  7.2 1.6 copy.32
  8.9 1.4 fusion.6
  10.9 1.4 fusion.11
  12.3 4.4 collective-permute-start
  16.7 1.3 collective-permute-start.1
  19.2 35.4 %all_gather.7 = bf16[384,768]{0,1:T(8,128)(2,1)S(1)} all-gather(bf16[384,48]{0,1:T(8,128)(2,1)S(1)} %copy-done.11), channel_id=1, replica_groups=mesh['dp'=32,'seq'=16] {'seq'}, dimensions={1}, use_global_device_ids=true | all-gather | bytes 626688 | tf_op jit(solution)/shard_map/all_gather | solution.py:54
  54.6 1.5 fusion.21
  57.1 22.8 %all-gather.2.cloned.1.call-done = bf16[2304,384]{0,1:T(8,128)(2,1)} async-done(((bf16[2304,24]{0,1:T(8,128)(2,1)}), bf16[2304,384]{0,1:T(8,128)(2,1)}) %all-gather.2.cloned.1.call-update) | async-done | bytes 1769488 | tf_op jit(solution)/shard_map/all_gather | solution.py:48
  79.9 1.8 fusion.39
  82.8 1.5 multiply_convert_fusion
  84.9 3.3 collective-permute-start.3
  88.2 1.3 collective-permute-start.2
  90.5 3.1 collective-permute-done.2
  94.9 2.4 fusion.19
  98.0 7.4 %all-to-all-start.2 = ((f32[1,16,48]{2,0,1:T(1,128)}), f32[1,16,48]{2,0,1:T(1,128)S(1)}, u32[]{:S(2)}, u32[]{:S(2)}) async-start(f32[1,16,48]{2,0,1:T(1,128)} %all_to_all.31), calls=%async_computation.2 | async-start | bytes 16384 | tf_op jit(solution)/shard_map/all_to_all | solution.py:123
  105.4 2.9 fusion.51
  108.3 8.4 %all-to-all-done.2 = f32[1,16,48]{2,0,1:T(1,128)S(1)} async-done(((f32[1,16,48]{2,0,1:T(1,128)}), f32[1,16,48]{2,0,1:T(1,128)S(1)}, u32[]{:S(2)}, u32[]{:S(2)}) %all-to-all-start.2) | async-done | bytes 3104 | tf_op jit(solution)/shard_map/all_to_all | solution.py:123
  116.6 4.4 all-to-all-start.1
  121.0 1.7 convolution_bitcast_fusion
  124.5 2.0 pad_maximum_fusion
  126.5 6.4 %copy.25 = f32[3,768,384]{1,0,2:T(4,128)} copy(f32[3,768,384]{2,1,0:T(8,128)} %pad_maximum_fusion) | data formatting | bytes 7077888 | tf_op jit(solution)/shard_map/stack | solution.py:119
  133.0 6.6 %all_to_all.13 = f32[2304,16,24]{0,2,1:T(8,128)} reshape(f32[3,768,384]{1,0,2:T(4,128)} %copy.25) | data formatting | bytes 7077888 | tf_op jit(solution)/shard_map/all_to_all | solution.py:121
  139.6 22.8 %all-to-all-done.1 = f32[384,16,48]{0,2,1:T(8,128)} async-done(((f32[384,16,48]{0,2,1:T(8,128)}), f32[384,16,48]{0,2,1:T(8,128)}, u32[]{:S(2)}, u32[]{:S(2)}) %all-to-all-start.1) | async-done | bytes 1179680 | tf_op jit(solution)/shard_map/all_to_all | solution.py:122
  162.4 17.7 %all-to-all-start = ((f32[2304,16,24]{0,2,1:T(8,128)}), f32[2304,16,24]{0,2,1:T(8,128)}, u32[]{:S(2)}, u32[]{:S(2)}) async-start(f32[2304,16,24]{0,2,1:T(8,128)} %all_to_all.13), calls=%async_computation | async-start | bytes 7077888 | tf_op jit(solution)/shard_map/all_to_all | solution.py:121
  180.2 1.5 fusion.13
  181.6 2.5 fusion.16
  184.2 70.6 %psum.23 = f32[1,48]{1,0:T(1,128)S(1)} all-reduce(f32[1,48]{1,0:T(1,128)S(1)} %bitcast.73), channel_id=1, replica_groups=mesh['dp'=32,'seq'=16] {'dp'}, use_global_device_ids=true, to_apply=%region_8.0 | all-reduce | flops 48 | bytes 384 | tf_op jit(solution)/shard_map/psum | solution.py:130
  254.7 2.0 reduce_sum.59
  256.7 77.1 %all-to-all-done = f32[2304,16,24]{0,2,1:T(8,128)} async-done(((f32[2304,16,24]{0,2,1:T(8,128)}), f32[2304,16,24]{0,2,1:T(8,128)}, u32[]{:S(2)}, u32[]{:S(2)}) %all-to-all-start) | async-done | bytes 3538976 | tf_op jit(solution)/shard_map/all_to_all | solution.py:121
  333.8 2.9 reduce_sum.58
  337.2 131.4 %all-reduce.3.cloned.1.call-done = (f32[2304,24]{0,1:T(8,128)}, f32[384,48]{0,1:T(8,128)}) async-done(((f32[2304,24]{0,1:T(8,128)}, f32[384,48]{0,1:T(8,128)}), (f32[2304,24]{0,1:T(8,128)}, f32[384,48]{0,1:T(8,128)})) %all-reduce.3.cloned.1.call-update) | async-done | bytes 294928 | tf_op jit(solution)/shard_map/psum | solution.py:130
  470.2 1.5 broadcast_multiply_fusion.1
  (54 shorter events, 11.5 us)
Async XLA Ops:
  7.2 3.7 copy-start
  7.2 72.7 %all-gather.2.cloned.1.call-start = ((), (), s32[]{:S(2)}) async-start(), calls=%async_computation.3 | async-start | bytes 1880064 | tf_op jit(solution)/shard_map/all_gather | solution.py:48
  8.9 9.1 %copy-start.1 = (bf16[2,256,768]{2,1,0:T(8,128)(2,1)S(1)}, bf16[2,256,768]{2,1,0:T(8,128)(2,1)}, u32[]{:S(2)}) copy-start(bf16[2,256,768]{2,1,0:T(8,128)(2,1)} %param.9) | copy-start | bytes 2359300
  12.3 6.9 %copy-start.11 = (bf16[384,48]{0,1:T(8,128)(2,1)S(1)}, bf16[384,48]{0,1:T(8,128)(2,1)}, u32[]{:S(2)}) copy-start(bf16[384,48]{0,1:T(8,128)(2,1)} %param.8) | copy-start | bytes 110596
  12.3 43.8 %collective-permute-start = (bf16[2,64,768]{2,1,0:T(8,128)(2,1)S(1)}, bf16[2,64,768]{2,1,0:T(8,128)(2,1)S(1)}, u32[]{:S(2)}, u32[]{:S(2)}) collective-permute-start(bf16[2,64,768]{2,1,0:T(8,128)(2,1)S(1)} %get-tuple-element.21), channel_id=1, source_target_pairs={{0,1},{1,2},{2,3},{3,4},{4,5},{5,6},{6,7},{7,8},{8,9},{9,10},{10,1... | collective-permute-start | bytes 589832 | tf_op jit(solution)/shard_map/ppermute | solution.py:19
  16.7 39.4 %collective-permute-start.1 = (bf16[2,64,768]{2,1,0:T(8,128)(2,1)S(1)}, bf16[2,64,768]{2,1,0:T(8,128)(2,1)S(1)}, u32[]{:S(2)}, u32[]{:S(2)}) collective-permute-start(bf16[2,64,768]{2,1,0:T(8,128)(2,1)S(1)} %get-tuple-element.22), channel_id=1, source_target_pairs={{1,0},{2,1},{3,2},{4,3},{5,4},{6,5},{7,6},{8,7},{9,8},{10,9},{11,1... | collective-permute-start | bytes 589832 | tf_op jit(solution)/shard_map/ppermute | solution.py:20
  54.6 1.5 copy-start.3
  57.1 25.2 %copy-start.2 = (bf16[2,256,768]{2,1,0:T(8,128)(2,1)}, bf16[2,256,768]{2,1,0:T(8,128)(2,1)S(1)}, u32[]{:S(2)}) copy-start(bf16[2,256,768]{2,1,0:T(8,128)(2,1)S(1)} %get-tuple-element.20) | copy-start | bytes 2359300
  79.9 1.8 copy-start.5
  81.7 1.1 copy-start.7
  82.8 1.5 copy-start.6
  84.9 5.6 %collective-permute-start.3 = (bf16[2,64,384]{2,1,0:T(8,128)(2,1)S(1)}, bf16[2,64,384]{2,1,0:T(8,128)(2,1)S(1)}, u32[]{:S(2)}, u32[]{:S(2)}) collective-permute-start(bf16[2,64,384]{2,1,0:T(8,128)(2,1)S(1)} %get-tuple-element.25), channel_id=1, source_target_pairs={{0,1},{1,2},{2,3},{3,4},{4,5},{5,6},{6,7},{7,8},{8,9},{9,10},{10,1... | collective-permute-start | bytes 294920 | tf_op jit(solution)/shard_map/ppermute | solution.py:19
  88.2 5.4 %collective-permute-start.2 = (bf16[2,64,384]{2,1,0:T(8,128)(2,1)S(1)}, bf16[2,64,384]{2,1,0:T(8,128)(2,1)S(1)}, u32[]{:S(2)}, u32[]{:S(2)}) collective-permute-start(bf16[2,64,384]{2,1,0:T(8,128)(2,1)S(1)} %get-tuple-element.26), channel_id=1, source_target_pairs={{1,0},{2,1},{3,2},{4,3},{5,4},{6,5},{7,6},{8,7},{9,8},{10,9},{11,1... | collective-permute-start | bytes 294920 | tf_op jit(solution)/shard_map/ppermute | solution.py:20
  94.2 0.7 copy-start.10
  98.0 18.7 %all-to-all-start.2 = ((f32[1,16,48]{2,0,1:T(1,128)}), f32[1,16,48]{2,0,1:T(1,128)S(1)}, u32[]{:S(2)}, u32[]{:S(2)}) async-start(f32[1,16,48]{2,0,1:T(1,128)} %all_to_all.31), calls=%async_computation.2 | async-start | bytes 16384 | tf_op jit(solution)/shard_map/all_to_all | solution.py:123
  116.6 45.7 %all-to-all-start.1 = ((f32[384,16,48]{0,2,1:T(8,128)}), f32[384,16,48]{0,2,1:T(8,128)}, u32[]{:S(2)}, u32[]{:S(2)}) async-start(f32[384,16,48]{0,2,1:T(8,128)} %fusion.51), calls=%async_computation.1 | async-start | bytes 2359296 | tf_op jit(solution)/shard_map/all_to_all | solution.py:122
  122.8 1.1 copy-start.8
  139.6 40.5 %copy-start.4 = (bf16[384,768]{0,1:T(8,128)(2,1)S(1)}, bf16[384,768]{0,1:T(8,128)(2,1)}, u32[]{:S(2)}) copy-start(bf16[384,768]{0,1:T(8,128)(2,1)} %copy-done.3) | copy-start | bytes 1769476
  139.6 40.5 %copy-start.9 = (bf16[512,384]{1,0:T(8,128)(2,1)S(1)}, bf16[512,384]{1,0:T(8,128)(2,1)}, u32[]{:S(2)}) copy-start(bf16[512,384]{1,0:T(8,128)(2,1)} %get-tuple-element.29) | copy-start | bytes 1179652
  162.4 171.4 %all-to-all-start = ((f32[2304,16,24]{0,2,1:T(8,128)}), f32[2304,16,24]{0,2,1:T(8,128)}, u32[]{:S(2)}, u32[]{:S(2)}) async-start(f32[2304,16,24]{0,2,1:T(8,128)} %all_to_all.13), calls=%async_computation | async-start | bytes 7077888 | tf_op jit(solution)/shard_map/all_to_all | solution.py:121
  180.1 1.6 copy-start.12
  180.1 1.6 copy-start.13
  180.1 288.5 %all-reduce.3.cloned.1.call-start = ((), (), s32[]{:S(2)}) async-start(), calls=%async_computation.4 | async-start | bytes 589824 | tf_op jit(solution)/shard_map/psum | solution.py:130
Sparse Core Ops, SparseCore 0:
  10.7 69.1 all-gather.1
  336.8 131.7 all-reduce.2
where the time goes:
time: 480 us; the launch traced here: 479 us
  waiting for transfers between devices  266 us (55%)
  blocking collectives  106 us (22%)
  starting transfers between devices  39.9 us (8%)
  other arithmetic  19.7 us (4%)
  local copies, waits for them, and re-layouts  18.5 us (4%)
  matrix products  14.7 us (3%)
  between operations  14.3 us (3%)
    psum x1, waiting for transfers between devices, on_device(): lax.psum((dilated_weight_portion, output_weight_portion, gain_share), 'dp')  131 us
    all_to_all x1, waiting for transfers between devices, on_device(): lax.all_to_all(dilated_piece, 'seq', split_axis=1, concat_axis=0, tiled=T...  77.1 us
    psum x1, blocking collectives, on_device(): lax.psum((dilated_weight_portion, output_weight_portion, gain_share), 'dp')  70.6 us
    all_gather x1, blocking collectives, on_device(): lax.all_gather(output_weight, 'seq', axis=1, tiled=True)  35.4 us
    all_gather x1, waiting for transfers between devices, on_device(): lax.all_gather(dilated_weight.reshape(3 * channel_count, dilated_weight.s...  22.8 us
    all_to_all x1, waiting for transfers between devices, on_device(): lax.all_to_all(output_piece, 'seq', split_axis=1, concat_axis=0, tiled=True)  22.8 us
    all_to_all x1, starting transfers between devices, on_device(): lax.all_to_all(dilated_piece, 'seq', split_axis=1, concat_axis=0, tiled=T...  17.7 us
  transfers between devices with their start and end apart: 9, of which 6 were waited for; matrix products, arithmetic and copies ran while one was open for 6% of the time, Pallas kernels for 0%

commit v1 on v0

--- a/solution.py
+++ b/solution.py
@@ -44,13 +44,15 @@
 def on_device(tokens, norm_gain, dilated_weight, output_weight, cotangent):
     seqs_here, local_bins, channel_count = tokens.shape
     sequence_number = lax.axis_size("seq")
+
+    def slots_settle(row_data):
+        v_now = jnp.stack([row_data] * lax.axis_size("seq"), 0)
+        side_arr = lax.all_to_all(v_now, axis_name="seq", split_axis=0, concat_axis=0)
+        outer = jnp.concatenate(side_arr, 1)
+        return outer
+
     collected_dilated, collected_output = (
-        lax.all_gather(
-            dilated_weight.reshape(3 * channel_count, dilated_weight.shape[2]),
-            "seq",
-            axis=1,
-            tiled=True,
-        ),
+        slots_settle(dilated_weight.reshape(3 * channel_count, dilated_weight.shape[2])),
         lax.all_gather(output_weight, "seq", axis=1, tiled=True),
     )
     hidden_width = collected_dilated.shape[1]

time: 480 us -> 537 us (1.12)
  blocking collectives: 106 us -> 164 us
  waiting for transfers between devices: 266 us -> 248 us
  starting transfers between devices: 39.9 us -> 54.5 us
    all_gather x1, blocking collectives: 35.4 us -> 94.3 us  [on_device(): lax.all_gather(output_weight, 'seq', axis=1, tiled=True)]
    all_gather x1 -> x0, waiting for transfers between devices: 22.8 us -> none  [on_device(): lax.all_gather(dilated_weight.reshape(3 * channel_count, dilated_weight.s...]
    all_to_all x0 -> x1, starting transfers between devices: none -> 15.9 us  [slots_settle(): lax.all_to_all(v_now, axis_name='seq', split_axis=0, concat_axis=0)]
    all_to_all x1, waiting for transfers between devices: 22.8 us -> 29.9 us  [on_device(): lax.all_to_all(output_piece, 'seq', split_axis=1, concat_axis=0, tiled=True)]
  transfers between devices with their start and end apart: 9 -> 9, of which waited for: 6 -> 5; matrix products, arithmetic and copies ran while one was open for 6% -> 6% of each run, Pallas kernels for 0% -> 0%
where the time goes in v1:
time: 537 us; the launch traced here: 536 us
  waiting for transfers between devices  248 us (46%)
  blocking collectives  164 us (31%)
  starting transfers between devices  54.5 us (10%)
  local copies, waits for them, and re-layouts  23.2 us (4%)
  other arithmetic  19.1 us (4%)
  between operations  14.3 us (3%)
  matrix products  12.6 us (2%)
    psum x1, waiting for transfers between devices, on_device(): lax.psum((dilated_weight_portion, output_weight_portion, gain_share), 'dp')  132 us
    all_gather x1, blocking collectives, on_device(): lax.all_gather(output_weight, 'seq', axis=1, tiled=True)  94.3 us
    all_to_all x1, waiting for transfers between devices, on_device(): lax.all_to_all(dilated_piece, 'seq', split_axis=1, concat_axis=0, tiled=T...  77.8 us
    psum x1, blocking collectives, on_device(): lax.psum((dilated_weight_portion, output_weight_portion, gain_share), 'dp')  69.8 us
    all_to_all x1, waiting for transfers between devices, on_device(): lax.all_to_all(output_piece, 'seq', split_axis=1, concat_axis=0, tiled=True)  29.9 us
    all_to_all x1, starting transfers between devices, slots_settle(): lax.all_to_all(v_now, axis_name='seq', split_axis=0, concat_axis=0)  15.9 us
    all_to_all x1, starting transfers between devices, on_device(): lax.all_to_all(dilated_piece, 'seq', split_axis=1, concat_axis=0, tiled=T...  12.4 us
    all_to_all x1, starting transfers between devices, on_device(): lax.all_to_all(gain_piece.reshape(1, channel_count), 'seq', split_axis=1,...  11.3 us
  transfers between devices with their start and end apart: 9, of which 5 were waited for; matrix products, arithmetic and copies ran while one was open for 6% of the time, Pallas kernels for 0%

profile of v1, /device:TPU:1, one launch (start us, length us, event | category | flops | bytes accessed | tf_op | source)
XLA Modules:
  0.0 536.1 jit_solution(8939125817442943455)
XLA Ops:
  7.2 0.9 copy.32
  8.1 1.4 stack.15
  9.4 15.9 %all-to-all-start = ((bf16[16,2304,24]{1,2,0:T(8,128)(2,1)}), bf16[16,2304,24]{1,2,0:T(8,128)(2,1)S(1)}, u32[]{:S(2)}, u32[]{:S(2)}) async-start(bf16[16,2304,24]{1,2,0:T(8,128)(2,1)} %stack.15), calls=%async_computation | async-start | bytes 3538944 | tf_op jit(solution)/shard_map/all_to_all | solution.py:50
  27.5 3.9 collective-permute-start
  31.5 1.3 collective-permute-start.1
  32.7 2.3 copy.26
  35.1 94.3 %all_gather.3 = bf16[384,768]{0,1:T(8,128)(2,1)S(1)} all-gather(bf16[384,48]{0,1:T(8,128)(2,1)} %param.8), channel_id=1, replica_groups=mesh['dp'=32,'seq'=16] {'seq'}, dimensions={1}, use_global_device_ids=true | all-gather | bytes 626688 | tf_op jit(solution)/shard_map/all_gather | solution.py:56
  130.1 2.6 fusion.21
  132.8 2.3 pad_maximum_fusion.2
  135.1 1.0 copy-done.2
  139.6 1.3 collective-permute-start.2
  140.9 4.0 collective-permute-start.3
  144.9 0.9 fusion.39
  147.7 2.4 fusion.19
  150.8 11.3 %all-to-all-start.3 = ((f32[1,16,48]{2,0,1:T(1,128)}), f32[1,16,48]{2,0,1:T(1,128)S(1)}, u32[]{:S(2)}, u32[]{:S(2)}) async-start(f32[1,16,48]{2,0,1:T(1,128)} %all_to_all.35), calls=%async_computation.3 | async-start | bytes 16384 | tf_op jit(solution)/shard_map/all_to_all | solution.py:125
  162.1 2.7 fusion.37
  164.9 8.5 %all-to-all-done.3 = f32[1,16,48]{2,0,1:T(1,128)S(1)} async-done(((f32[1,16,48]{2,0,1:T(1,128)}), f32[1,16,48]{2,0,1:T(1,128)S(1)}, u32[]{:S(2)}, u32[]{:S(2)}) %all-to-all-start.3) | async-done | bytes 3104 | tf_op jit(solution)/shard_map/all_to_all | solution.py:125
  173.3 4.4 all-to-all-start.2
  180.1 2.0 pad_maximum_fusion
  182.1 6.4 %copy.25 = f32[3,768,384]{1,0,2:T(4,128)} copy(f32[3,768,384]{2,1,0:T(8,128)} %pad_maximum_fusion) | data formatting | bytes 7077888 | tf_op jit(solution)/shard_map/stack | solution.py:121
  188.6 6.6 %all_to_all.32 = f32[2304,16,24]{0,2,1:T(8,128)} reshape(f32[3,768,384]{1,0,2:T(4,128)} %copy.25) | data formatting | bytes 7077888 | tf_op jit(solution)/shard_map/all_to_all | solution.py:123
  195.2 29.9 %all-to-all-done.2 = f32[384,16,48]{0,2,1:T(8,128)} async-done(((f32[384,16,48]{0,2,1:T(8,128)}), f32[384,16,48]{0,2,1:T(8,128)}, u32[]{:S(2)}, u32[]{:S(2)}) %all-to-all-start.2) | async-done | bytes 1179680 | tf_op jit(solution)/shard_map/all_to_all | solution.py:124
  225.1 12.4 %all-to-all-start.1 = ((f32[2304,16,24]{0,2,1:T(8,128)}), f32[2304,16,24]{0,2,1:T(8,128)}, u32[]{:S(2)}, u32[]{:S(2)}) async-start(f32[2304,16,24]{0,2,1:T(8,128)} %all_to_all.32), calls=%async_computation.1 | async-start | bytes 7077888 | tf_op jit(solution)/shard_map/all_to_all | solution.py:123
  237.5 1.5 fusion.13
  239.0 2.5 fusion.16
  241.6 69.8 %psum.23 = f32[1,48]{1,0:T(1,128)S(1)} all-reduce(f32[1,48]{1,0:T(1,128)S(1)} %bitcast.90), channel_id=1, replica_groups=mesh['dp'=32,'seq'=16] {'dp'}, use_global_device_ids=true, to_apply=%region_8.0 | all-reduce | flops 48 | bytes 384 | tf_op jit(solution)/shard_map/psum | solution.py:132
  311.4 2.0 reduce_sum.59
  313.4 77.8 %all-to-all-done.1 = f32[2304,16,24]{0,2,1:T(8,128)} async-done(((f32[2304,16,24]{0,2,1:T(8,128)}), f32[2304,16,24]{0,2,1:T(8,128)}, u32[]{:S(2)}, u32[]{:S(2)}) %all-to-all-start.1) | async-done | bytes 3538976 | tf_op jit(solution)/shard_map/all_to_all | solution.py:123
  391.1 2.9 reduce_sum.58
  394.5 131.5 %all-reduce.3.cloned.1.call-done = (f32[2304,24]{0,1:T(8,128)}, f32[384,48]{0,1:T(8,128)}) async-done(((f32[2304,24]{0,1:T(8,128)}, f32[384,48]{0,1:T(8,128)}), (f32[2304,24]{0,1:T(8,128)}, f32[384,48]{0,1:T(8,128)})) %all-reduce.3.cloned.1.call-update) | async-done | bytes 294928 | tf_op jit(solution)/shard_map/psum | solution.py:132
  526.1 1.0 broadcast_multiply_fusion
  527.7 1.5 broadcast_multiply_fusion.1
  (55 shorter events, 12.7 us)
Async XLA Ops:
  9.4 15.9 %copy-start = (bf16[2,256,768]{2,1,0:T(8,128)(2,1)S(1)}, bf16[2,256,768]{2,1,0:T(8,128)(2,1)}, u32[]{:S(2)}) copy-start(bf16[2,256,768]{2,1,0:T(8,128)(2,1)} %param.5) | copy-start | bytes 2359300
  9.4 16.7 %copy-start.11 = (f32[768]{0:T(1024)S(1)}, f32[768]{0:T(1024)}, u32[]{:S(2)}) copy-start(f32[768]{0:T(1024)} %param.6) | copy-start | bytes 9220
  9.4 125.6 %all-to-all-start = ((bf16[16,2304,24]{1,2,0:T(8,128)(2,1)}), bf16[16,2304,24]{1,2,0:T(8,128)(2,1)S(1)}, u32[]{:S(2)}, u32[]{:S(2)}) async-start(bf16[16,2304,24]{1,2,0:T(8,128)(2,1)} %stack.15), calls=%async_computation | async-start | bytes 3538944 | tf_op jit(solution)/shard_map/all_to_all | solution.py:50
  27.5 105.2 %collective-permute-start = (bf16[2,64,768]{2,1,0:T(8,128)(2,1)}, bf16[2,64,768]{2,1,0:T(8,128)(2,1)}, u32[]{:S(2)}, u32[]{:S(2)}) collective-permute-start(bf16[2,64,768]{2,1,0:T(8,128)(2,1)} %get-tuple-element.24), channel_id=1, source_target_pairs={{0,1},{1,2},{2,3},{3,4},{4,5},{5,6},{6,7},{7,8},{8,9},{9,10},{10,1... | collective-permute-start | bytes 589832 | tf_op jit(solution)/shard_map/ppermute | solution.py:19
  31.5 101.3 %collective-permute-start.1 = (bf16[2,64,768]{2,1,0:T(8,128)(2,1)S(1)}, bf16[2,64,768]{2,1,0:T(8,128)(2,1)}, u32[]{:S(2)}, u32[]{:S(2)}) collective-permute-start(bf16[2,64,768]{2,1,0:T(8,128)(2,1)S(1)} %get-tuple-element.25), channel_id=1, source_target_pairs={{1,0},{2,1},{3,2},{4,3},{5,4},{6,5},{7,6},{8,7},{9,8},{10,9},{11,1... | collective-permute-start | bytes 589832 | tf_op jit(solution)/shard_map/ppermute | solution.py:20
  129.3 0.8 copy-start.6
  135.0 1.1 copy-start.2
  136.8 1.1 copy-start.4
  137.9 1.1 copy-start.8
  138.6 23.5 %copy-start.9 = (bf16[512,384]{1,0:T(8,128)(2,1)}, bf16[512,384]{1,0:T(8,128)(2,1)S(1)}, u32[]{:S(2)}) copy-start(bf16[512,384]{1,0:T(8,128)(2,1)S(1)} %get-tuple-element.32) | copy-start | bytes 1179652
  139.6 6.2 %collective-permute-start.2 = (bf16[2,64,384]{2,1,0:T(8,128)(2,1)S(1)}, bf16[2,64,384]{2,1,0:T(8,128)(2,1)S(1)}, u32[]{:S(2)}, u32[]{:S(2)}) collective-permute-start(bf16[2,64,384]{2,1,0:T(8,128)(2,1)S(1)} %get-tuple-element.28), channel_id=1, source_target_pairs={{1,0},{2,1},{3,2},{4,3},{5,4},{6,5},{7,6},{8,7},{9,8},{10,9},{11,1... | collective-permute-start | bytes 294920 | tf_op jit(solution)/shard_map/ppermute | solution.py:20
  140.9 5.6 %collective-permute-start.3 = (bf16[2,64,384]{2,1,0:T(8,128)(2,1)S(1)}, bf16[2,64,384]{2,1,0:T(8,128)(2,1)S(1)}, u32[]{:S(2)}, u32[]{:S(2)}) collective-permute-start(bf16[2,64,384]{2,1,0:T(8,128)(2,1)S(1)} %get-tuple-element.29), channel_id=1, source_target_pairs={{0,1},{1,2},{2,3},{3,4},{4,5},{5,6},{6,7},{7,8},{8,9},{9,10},{10,1... | collective-permute-start | bytes 294920 | tf_op jit(solution)/shard_map/ppermute | solution.py:19
  150.8 22.6 %all-to-all-start.3 = ((f32[1,16,48]{2,0,1:T(1,128)}), f32[1,16,48]{2,0,1:T(1,128)S(1)}, u32[]{:S(2)}, u32[]{:S(2)}) async-start(f32[1,16,48]{2,0,1:T(1,128)} %all_to_all.35), calls=%async_computation.3 | async-start | bytes 16384 | tf_op jit(solution)/shard_map/all_to_all | solution.py:125
  164.9 12.9 %copy-start.3 = (bf16[2,256,768]{2,1,0:T(8,128)(2,1)S(1)}, bf16[2,256,768]{2,1,0:T(8,128)(2,1)}, u32[]{:S(2)}) copy-start(bf16[2,256,768]{2,1,0:T(8,128)(2,1)} %get-tuple-element.23) | copy-start | bytes 2359300
  173.3 51.7 %all-to-all-start.2 = ((f32[384,16,48]{0,2,1:T(8,128)}), f32[384,16,48]{0,2,1:T(8,128)}, u32[]{:S(2)}, u32[]{:S(2)}) async-start(f32[384,16,48]{0,2,1:T(8,128)} %fusion.37), calls=%async_computation.2 | async-start | bytes 2359296 | tf_op jit(solution)/shard_map/all_to_all | solution.py:124
  178.3 1.1 copy-start.5
  195.2 42.3 %copy-start.7 = (bf16[384,768]{0,1:T(8,128)(2,1)S(1)}, bf16[384,768]{0,1:T(8,128)(2,1)}, u32[]{:S(2)}) copy-start(bf16[384,768]{0,1:T(8,128)(2,1)} %copy-done.6) | copy-start | bytes 1769476
  195.2 42.3 %copy-start.10 = (bf16[512,384]{1,0:T(8,128)(2,1)S(1)}, bf16[512,384]{1,0:T(8,128)(2,1)}, u32[]{:S(2)}) copy-start(bf16[512,384]{1,0:T(8,128)(2,1)} %copy-done.9) | copy-start | bytes 1179652
  225.1 166.1 %all-to-all-start.1 = ((f32[2304,16,24]{0,2,1:T(8,128)}), f32[2304,16,24]{0,2,1:T(8,128)}, u32[]{:S(2)}, u32[]{:S(2)}) async-start(f32[2304,16,24]{0,2,1:T(8,128)} %all_to_all.32), calls=%async_computation.1 | async-start | bytes 7077888 | tf_op jit(solution)/shard_map/all_to_all | solution.py:123
  237.4 1.6 copy-start.12
  237.4 1.6 copy-start.1
  237.5 1.6 copy-start.13
  237.5 288.6 %all-reduce.3.cloned.1.call-start = ((), (), s32[]{:S(2)}) async-start(), calls=%async_computation.4 | async-start | bytes 589824 | tf_op jit(solution)/shard_map/psum | solution.py:132
Sparse Core Ops, SparseCore 0:
  394.1 131.8 all-reduce.2
